TPU v7x, 512 devices: a whole 4x4x16 slice. The times are simulated.
512 devices in a mesh: grp: 16 (over z), sub: 32 (over x, y, core).
Axes of the slice: x: 4, y: 4, z: 16, core: 2. Of those that a mesh axis runs over, the one named last changes fastest.
Arguments:
- top_basis: bfloat16 [16, 512, 256], P('grp', 'sub'), may hold values from -0.375 to 0.375
- top_coeffs: bfloat16 [16, 256, 128], P('grp'), may hold values from -6 to 6
- top_coupling: float32 [16, 512, 512], P('grp')
- block_coupling: float32 [16, 32, 128, 512], P('grp', 'sub'), may hold values from -0.09375 to 0.09375
- block_basis: bfloat16 [16, 32, 128, 128], P('grp', 'sub'), may hold values from -0.5 to 0.5
- block_coeffs: bfloat16 [16, 32, 128, 128], P('grp', 'sub'), may hold values from -6 to 6
- sub_basis: bfloat16 [16, 32, 1536, 256], P('grp', 'sub'), may hold values from -0.375 to 0.375
- sub_coeffs: bfloat16 [16, 32, 256, 128], P('grp', 'sub'), may hold values from -6 to 6
- basis_widths: int32 [16, 32], P('grp', 'sub'), may hold values from 32 to 256
- constraint_modes: bfloat16 [16, 32, 1536, 512], P('grp', 'sub'), may hold values from -0.25 to 0.25
- adjacency: int32 [16, 32, 4], P('grp', 'sub'), may hold values from 0 to 4, as said below
Outputs:
- top_values: float32 [16, 512, 128], P('grp')
- block_values: bfloat16 [16, 32, 128, 128], P('grp', 'sub')
- interior: bfloat16 [16, 32, 1536, 128], P('grp', 'sub')
Inputs may be any that keep to these rules, and one draw needn't show every extreme that they name: `adjacency`: the 4 entries of one substructure are different.
All inputs are finite; a program needn't handle non-finite values.
Results may differ from a plain program's by a relative error of at most 0.0044.
Values may be sent and summed in bfloat16 or wider, within the bound.
No kernel may reach another device: no remote copies, remote signals or barrier semaphores. Data moves between devices by JAX's collectives and lax.ppermute only.
A program may use at most 64 MiB of HBM per device.

v0:
```python
import jax
import jax.numpy as jnp
from jax import lax
from jax.sharding import PartitionSpec as P


def from_behind(shard, axis, by):
    peers = lax.axis_size(axis)
    return lax.ppermute(shard, axis, [(i, (i + by) % peers) for i in range(peers)])


def from_behind_2(value, axis, steps):
    count = lax.axis_size(axis)
    first, last = (max(0, -steps), min(count, count - steps))
    return lax.ppermute(value, axis, [(source, source + steps) for source in range(first, last)])


def neighbour_block(block, offset):
    return from_behind(block, "sub", -offset)


def run_chain(top_own, chain_matrix):
    highest = lax.Precision.HIGHEST

    def relay(turn_index, current):
        earlier = from_behind_2(current, "grp", 1)
        return top_own + jnp.dot(chain_matrix, earlier, precision=highest)

    return lax.fori_loop(0, lax.axis_size("grp"), relay, jnp.zeros_like(top_own))


def body(
    top_basis,
    top_coeffs,
    top_coupling,
    block_coupling,
    block_basis,
    block_coeffs,
    sub_basis,
    sub_coeffs,
    basis_widths,
    constraint_modes,
    adjacency,
):
    highest = lax.Precision.HIGHEST
    rows_own = jnp.dot(top_basis[0], top_coeffs[0], preferred_element_type=jnp.float32)
    chain_matrix = top_coupling[0]
    top_own = lax.all_gather(rows_own, "sub", axis=0, tiled=True)
    top_field = run_chain(top_own, chain_matrix)
    own_block = jnp.dot(block_basis[0, 0], block_coeffs[0, 0], preferred_element_type=jnp.float32)
    from_top = jnp.dot(block_coupling[0, 0], top_field, precision=highest)
    block = (own_block + from_top).astype(jnp.bfloat16)
    records = [block, block, block, block, block]
    for offset in (-2, -1, 1, 2):
        records[offset + 2] = neighbour_block(block, offset)
    candidates = jnp.stack(records)
    slots = adjacency[0, 0]
    chosen = jnp.take(candidates, slots, axis=0)
    linked = chosen.reshape(slots.shape[0] * block.shape[0], block.shape[1])
    bound_part = jnp.dot(constraint_modes[0, 0], linked, preferred_element_type=jnp.float32)
    kept_width = basis_widths[0, 0]
    coeffs = sub_coeffs[0, 0]
    basis = sub_basis[0, 0]
    width_total = coeffs.shape[0]
    live_mask = lax.broadcasted_iota(jnp.int32, (width_total, 1), 0) < kept_width
    live_coeffs = jnp.where(live_mask, coeffs, jnp.zeros_like(coeffs))
    fixed_part = jnp.dot(basis, live_coeffs, preferred_element_type=jnp.float32)
    interior = (fixed_part + bound_part).astype(jnp.bfloat16)
    return (top_field[None], block[None, None], interior[None, None])


def solution(mesh):
    placed = (
        P("grp", "sub", None),
        P("grp", None, None),
        P("grp", None, None),
        P("grp", "sub", None, None),
        P("grp", "sub", None, None),
        P("grp", "sub", None, None),
        P("grp", "sub", None, None),
        P("grp", "sub", None, None),
        P("grp", "sub"),
        P("grp", "sub", None, None),
        P("grp", "sub", None),
    )
    return jax.shard_map(
        body,
        mesh=mesh,
        in_specs=placed,
        out_specs=(P("grp", None, None), P("grp", "sub", None, None), P("grp", "sub", None, None)),
        check_vma=False,
    )
```

profile of v0, /device:TPU:384, one launch (start us, length us, event | category | flops | bytes accessed | tf_op | source)
XLA Modules:
  0.0 249.1 jit_solution(1026725116123611253)
XLA Ops:
  1.8 25.2 %all_gather.3 = f32[512,128]{1,0:T(8,128)S(1)} all-gather(f32[16,128]{1,0:T(8,128)S(1)} %fusion.8), channel_id=1, replica_groups=mesh['grp'=16,'sub'=32] {'sub'}, dimensions={0}, use_global_device_ids=true | all-gather | bytes 270336 | tf_op jit(solution)/shard_map/all_gather | solution.py:48
  26.9 199.4 %while.11 = (s32[]{:T(128)}, f32[512,128]{1,0:T(8,128)S(1)}, f32[512,512]{1,0:T(8,128)}, f32[512,128]{1,0:T(8,128)S(1)}, s32[]{:T(128)}, /*index=5*/s32[]{:T(128)}) while((s32[]{:T(128)}, f32[512,128]{1,0:T(8,128)S(1)}, f32[512,512]{1,0:T(8,128)}, f32[512,128]{1,0:T(8,128)S(1)}, s32[]{:T(128)}, /*index=5*/s32[]{:T(128)}) %tuple.30), condition=%wide.region_1.0_spmd.clone, body=%wide.region_0.0_spmd.clone.sunk | while | flops 402784256 | bytes 3407991 | solution.py:29
  27.0 3.1 %collective-permute-start = (f32[512,128]{1,0:T(8,128)S(1)}, f32[512,128]{1,0:T(8,128)S(1)}, u32[]{:S(2)}, u32[]{:S(2)}) collective-permute-start(f32[512,128]{1,0:T(8,128)S(1)} %broadcast_select_fusion.3), channel_id=1, source_target_pairs={{0,32},{32,64},{64,96},{96,128},{128,160},{160,192},{192,224},{224... | collective-permute-start | bytes 786440 | tf_op jit(solution)/shard_map/while/body/eval_jaxpr/ppermute | solution.py:15
  30.0 8.8 %collective-permute-done = f32[512,128]{1,0:T(8,128)S(1)} collective-permute-done((f32[512,128]{1,0:T(8,128)S(1)}, f32[512,128]{1,0:T(8,128)S(1)}, u32[]{:S(2)}, u32[]{:S(2)}) %collective-permute-start) | collective-permute-done | bytes 262176 | tf_op jit(solution)/shard_map/while/body/eval_jaxpr/ppermute | solution.py:15
  38.8 2.2 convolution_add_fusion.4
  41.0 1.9 collective-permute-start
  43.0 8.9 %collective-permute-done = f32[512,128]{1,0:T(8,128)S(1)} collective-permute-done((f32[512,128]{1,0:T(8,128)S(1)}, f32[512,128]{1,0:T(8,128)S(1)}, u32[]{:S(2)}, u32[]{:S(2)}) %collective-permute-start) | collective-permute-done | bytes 262176 | tf_op jit(solution)/shard_map/while/body/eval_jaxpr/ppermute | solution.py:15
  51.9 2.2 convolution_add_fusion.4
  54.1 1.9 collective-permute-start
  56.1 8.0 %collective-permute-done = f32[512,128]{1,0:T(8,128)S(1)} collective-permute-done((f32[512,128]{1,0:T(8,128)S(1)}, f32[512,128]{1,0:T(8,128)S(1)}, u32[]{:S(2)}, u32[]{:S(2)}) %collective-permute-start) | collective-permute-done | bytes 262176 | tf_op jit(solution)/shard_map/while/body/eval_jaxpr/ppermute | solution.py:15
  64.1 2.2 convolution_add_fusion.4
  66.4 1.9 collective-permute-start
  68.3 7.5 %collective-permute-done = f32[512,128]{1,0:T(8,128)S(1)} collective-permute-done((f32[512,128]{1,0:T(8,128)S(1)}, f32[512,128]{1,0:T(8,128)S(1)}, u32[]{:S(2)}, u32[]{:S(2)}) %collective-permute-start) | collective-permute-done | bytes 262176 | tf_op jit(solution)/shard_map/while/body/eval_jaxpr/ppermute | solution.py:15
  75.9 2.2 convolution_add_fusion.4
  78.1 1.9 collective-permute-start
  80.0 7.5 %collective-permute-done = f32[512,128]{1,0:T(8,128)S(1)} collective-permute-done((f32[512,128]{1,0:T(8,128)S(1)}, f32[512,128]{1,0:T(8,128)S(1)}, u32[]{:S(2)}, u32[]{:S(2)}) %collective-permute-start) | collective-permute-done | bytes 262176 | tf_op jit(solution)/shard_map/while/body/eval_jaxpr/ppermute | solution.py:15
  87.6 2.2 convolution_add_fusion.4
  89.9 1.9 collective-permute-start
  91.8 7.5 %collective-permute-done = f32[512,128]{1,0:T(8,128)S(1)} collective-permute-done((f32[512,128]{1,0:T(8,128)S(1)}, f32[512,128]{1,0:T(8,128)S(1)}, u32[]{:S(2)}, u32[]{:S(2)}) %collective-permute-start) | collective-permute-done | bytes 262176 | tf_op jit(solution)/shard_map/while/body/eval_jaxpr/ppermute | solution.py:15
  99.3 2.2 convolution_add_fusion.4
  101.6 1.9 collective-permute-start
  103.5 7.5 %collective-permute-done = f32[512,128]{1,0:T(8,128)S(1)} collective-permute-done((f32[512,128]{1,0:T(8,128)S(1)}, f32[512,128]{1,0:T(8,128)S(1)}, u32[]{:S(2)}, u32[]{:S(2)}) %collective-permute-start) | collective-permute-done | bytes 262176 | tf_op jit(solution)/shard_map/while/body/eval_jaxpr/ppermute | solution.py:15
  111.1 2.2 convolution_add_fusion.4
  113.3 1.9 collective-permute-start
  115.3 7.6 %collective-permute-done = f32[512,128]{1,0:T(8,128)S(1)} collective-permute-done((f32[512,128]{1,0:T(8,128)S(1)}, f32[512,128]{1,0:T(8,128)S(1)}, u32[]{:S(2)}, u32[]{:S(2)}) %collective-permute-start) | collective-permute-done | bytes 262176 | tf_op jit(solution)/shard_map/while/body/eval_jaxpr/ppermute | solution.py:15
  122.8 2.2 convolution_add_fusion.4
  127.0 8.7 %collective-permute-done = f32[512,128]{1,0:T(8,128)S(1)} collective-permute-done((f32[512,128]{1,0:T(8,128)S(1)}, f32[512,128]{1,0:T(8,128)S(1)}, u32[]{:S(2)}, u32[]{:S(2)}) %collective-permute-start) | collective-permute-done | bytes 262176 | tf_op jit(solution)/shard_map/while/body/eval_jaxpr/ppermute | solution.py:15
  135.7 2.2 convolution_add_fusion.4
  138.0 1.9 collective-permute-start
  139.9 9.9 %collective-permute-done = f32[512,128]{1,0:T(8,128)S(1)} collective-permute-done((f32[512,128]{1,0:T(8,128)S(1)}, f32[512,128]{1,0:T(8,128)S(1)}, u32[]{:S(2)}, u32[]{:S(2)}) %collective-permute-start) | collective-permute-done | bytes 262176 | tf_op jit(solution)/shard_map/while/body/eval_jaxpr/ppermute | solution.py:15
  149.7 2.2 convolution_add_fusion.4
  153.9 9.7 %collective-permute-done = f32[512,128]{1,0:T(8,128)S(1)} collective-permute-done((f32[512,128]{1,0:T(8,128)S(1)}, f32[512,128]{1,0:T(8,128)S(1)}, u32[]{:S(2)}, u32[]{:S(2)}) %collective-permute-start) | collective-permute-done | bytes 262176 | tf_op jit(solution)/shard_map/while/body/eval_jaxpr/ppermute | solution.py:15
  163.6 2.2 convolution_add_fusion.4
  167.8 8.9 %collective-permute-done = f32[512,128]{1,0:T(8,128)S(1)} collective-permute-done((f32[512,128]{1,0:T(8,128)S(1)}, f32[512,128]{1,0:T(8,128)S(1)}, u32[]{:S(2)}, u32[]{:S(2)}) %collective-permute-start) | collective-permute-done | bytes 262176 | tf_op jit(solution)/shard_map/while/body/eval_jaxpr/ppermute | solution.py:15
  176.7 2.2 convolution_add_fusion.4
  179.0 1.9 collective-permute-start
  180.9 8.0 %collective-permute-done = f32[512,128]{1,0:T(8,128)S(1)} collective-permute-done((f32[512,128]{1,0:T(8,128)S(1)}, f32[512,128]{1,0:T(8,128)S(1)}, u32[]{:S(2)}, u32[]{:S(2)}) %collective-permute-start) | collective-permute-done | bytes 262176 | tf_op jit(solution)/shard_map/while/body/eval_jaxpr/ppermute | solution.py:15
  188.9 2.2 convolution_add_fusion.4
  193.1 7.5 %collective-permute-done = f32[512,128]{1,0:T(8,128)S(1)} collective-permute-done((f32[512,128]{1,0:T(8,128)S(1)}, f32[512,128]{1,0:T(8,128)S(1)}, u32[]{:S(2)}, u32[]{:S(2)}) %collective-permute-start) | collective-permute-done | bytes 262176 | tf_op jit(solution)/shard_map/while/body/eval_jaxpr/ppermute | solution.py:15
  200.6 2.2 convolution_add_fusion.4
  202.9 1.9 collective-permute-start
  204.8 7.5 %collective-permute-done = f32[512,128]{1,0:T(8,128)S(1)} collective-permute-done((f32[512,128]{1,0:T(8,128)S(1)}, f32[512,128]{1,0:T(8,128)S(1)}, u32[]{:S(2)}, u32[]{:S(2)}) %collective-permute-start) | collective-permute-done | bytes 262176 | tf_op jit(solution)/shard_map/while/body/eval_jaxpr/ppermute | solution.py:15
  212.4 2.2 convolution_add_fusion.4
  216.5 7.5 %collective-permute-done = f32[512,128]{1,0:T(8,128)S(1)} collective-permute-done((f32[512,128]{1,0:T(8,128)S(1)}, f32[512,128]{1,0:T(8,128)S(1)}, u32[]{:S(2)}, u32[]{:S(2)}) %collective-permute-start) | collective-permute-done | bytes 262176 | tf_op jit(solution)/shard_map/while/body/eval_jaxpr/ppermute | solution.py:15
  224.1 2.2 convolution_add_fusion.4
  228.7 4.6 %collective-permute-start.4 = (bf16[128,128]{1,0:T(8,128)(2,1)S(1)}, bf16[128,128]{1,0:T(8,128)(2,1)S(1)}, u32[]{:S(2)}, u32[]{:S(2)}) collective-permute-start(bf16[128,128]{1,0:T(8,128)(2,1)S(1)} %fusion.3), channel_id=1, source_target_pairs={{0,30},{1,31},{2,0},{3,1},{4,2},{5,3},{6,4},{7,5},{8,6},{9,7},{10,... | collective-permute-start | bytes 98312 | tf_op jit(solution)/shard_map/ppermute | solution.py:9
  235.2 2.4 collective-permute-start.2
  240.8 6.0 %collective-permute-done.1 = bf16[128,128]{1,0:T(8,128)(2,1)S(1)} collective-permute-done((bf16[128,128]{1,0:T(8,128)(2,1)S(1)}, bf16[128,128]{1,0:T(8,128)(2,1)S(1)}, u32[]{:S(2)}, u32[]{:S(2)}) %collective-permute-start.1) | collective-permute-done | bytes 32800 | tf_op jit(solution)/shard_map/ppermute | solution.py:9
  (58 shorter events, 20.0 us)
Async XLA Ops:
  0.6 246.9 %copy-start = (bf16[1,1,1536,512]{3,2,1,0:T(8,128)(2,1)S(1)}, bf16[1,1,1536,512]{3,2,1,0:T(8,128)(2,1)}, u32[]{:S(2)}) copy-start(bf16[1,1,1536,512]{3,2,1,0:T(8,128)(2,1)} %param.22) | copy-start | bytes 4718596
  26.9 200.9 %copy-start.5 = (bf16[1,1,128,128]{3,2,1,0:T(8,128)(2,1)S(1)}, bf16[1,1,128,128]{3,2,1,0:T(8,128)(2,1)}, u32[]{:S(2)}) copy-start(bf16[1,1,128,128]{3,2,1,0:T(8,128)(2,1)} %param.18) | copy-start | bytes 98308
  26.9 212.7 %copy-start.6 = (s32[1,1,4]{2,1,0:T(1,128)S(1)}, s32[1,1,4]{2,1,0:T(1,128)}, u32[]{:S(2)}) copy-start(s32[1,1,4]{2,1,0:T(1,128)} %param.23) | copy-start | bytes 52
  26.9 213.4 %copy-start.2 = (bf16[1,1,1536,256]{3,2,1,0:T(8,128)(2,1)S(1)}, bf16[1,1,1536,256]{3,2,1,0:T(8,128)(2,1)}, u32[]{:S(2)}) copy-start(bf16[1,1,1536,256]{3,2,1,0:T(8,128)(2,1)} %param.19) | copy-start | bytes 2359300
  26.9 213.4 %copy-start.4 = (bf16[1,1,256,128]{3,2,1,0:T(8,128)(2,1)S(1)}, bf16[1,1,256,128]{3,2,1,0:T(8,128)(2,1)}, u32[]{:S(2)}) copy-start(bf16[1,1,256,128]{3,2,1,0:T(8,128)(2,1)} %param.20) | copy-start | bytes 196612
  27.0 11.8 %collective-permute-start = (f32[512,128]{1,0:T(8,128)S(1)}, f32[512,128]{1,0:T(8,128)S(1)}, u32[]{:S(2)}, u32[]{:S(2)}) collective-permute-start(f32[512,128]{1,0:T(8,128)S(1)} %broadcast_select_fusion.3), channel_id=1, source_target_pairs={{0,32},{32,64},{64,96},{96,128},{128,160},{160,192},{192,224},{224... | collective-permute-start | bytes 786440 | tf_op jit(solution)/shard_map/while/body/eval_jaxpr/ppermute | solution.py:15
  41.0 10.8 %collective-permute-start = (f32[512,128]{1,0:T(8,128)S(1)}, f32[512,128]{1,0:T(8,128)S(1)}, u32[]{:S(2)}, u32[]{:S(2)}) collective-permute-start(f32[512,128]{1,0:T(8,128)S(1)} %broadcast_select_fusion.3), channel_id=1, source_target_pairs={{0,32},{32,64},{64,96},{96,128},{128,160},{160,192},{192,224},{224... | collective-permute-start | bytes 786440 | tf_op jit(solution)/shard_map/while/body/eval_jaxpr/ppermute | solution.py:15
  54.1 10.0 %collective-permute-start = (f32[512,128]{1,0:T(8,128)S(1)}, f32[512,128]{1,0:T(8,128)S(1)}, u32[]{:S(2)}, u32[]{:S(2)}) collective-permute-start(f32[512,128]{1,0:T(8,128)S(1)} %broadcast_select_fusion.3), channel_id=1, source_target_pairs={{0,32},{32,64},{64,96},{96,128},{128,160},{160,192},{192,224},{224... | collective-permute-start | bytes 786440 | tf_op jit(solution)/shard_map/while/body/eval_jaxpr/ppermute | solution.py:15
  66.4 9.5 %collective-permute-start = (f32[512,128]{1,0:T(8,128)S(1)}, f32[512,128]{1,0:T(8,128)S(1)}, u32[]{:S(2)}, u32[]{:S(2)}) collective-permute-start(f32[512,128]{1,0:T(8,128)S(1)} %broadcast_select_fusion.3), channel_id=1, source_target_pairs={{0,32},{32,64},{64,96},{96,128},{128,160},{160,192},{192,224},{224... | collective-permute-start | bytes 786440 | tf_op jit(solution)/shard_map/while/body/eval_jaxpr/ppermute | solution.py:15
  78.1 9.5 %collective-permute-start = (f32[512,128]{1,0:T(8,128)S(1)}, f32[512,128]{1,0:T(8,128)S(1)}, u32[]{:S(2)}, u32[]{:S(2)}) collective-permute-start(f32[512,128]{1,0:T(8,128)S(1)} %broadcast_select_fusion.3), channel_id=1, source_target_pairs={{0,32},{32,64},{64,96},{96,128},{128,160},{160,192},{192,224},{224... | collective-permute-start | bytes 786440 | tf_op jit(solution)/shard_map/while/body/eval_jaxpr/ppermute | solution.py:15
  89.9 9.5 %collective-permute-start = (f32[512,128]{1,0:T(8,128)S(1)}, f32[512,128]{1,0:T(8,128)S(1)}, u32[]{:S(2)}, u32[]{:S(2)}) collective-permute-start(f32[512,128]{1,0:T(8,128)S(1)} %broadcast_select_fusion.3), channel_id=1, source_target_pairs={{0,32},{32,64},{64,96},{96,128},{128,160},{160,192},{192,224},{224... | collective-permute-start | bytes 786440 | tf_op jit(solution)/shard_map/while/body/eval_jaxpr/ppermute | solution.py:15
  101.6 9.5 %collective-permute-start = (f32[512,128]{1,0:T(8,128)S(1)}, f32[512,128]{1,0:T(8,128)S(1)}, u32[]{:S(2)}, u32[]{:S(2)}) collective-permute-start(f32[512,128]{1,0:T(8,128)S(1)} %broadcast_select_fusion.3), channel_id=1, source_target_pairs={{0,32},{32,64},{64,96},{96,128},{128,160},{160,192},{192,224},{224... | collective-permute-start | bytes 786440 | tf_op jit(solution)/shard_map/while/body/eval_jaxpr/ppermute | solution.py:15
  113.3 9.5 %collective-permute-start = (f32[512,128]{1,0:T(8,128)S(1)}, f32[512,128]{1,0:T(8,128)S(1)}, u32[]{:S(2)}, u32[]{:S(2)}) collective-permute-start(f32[512,128]{1,0:T(8,128)S(1)} %broadcast_select_fusion.3), channel_id=1, source_target_pairs={{0,32},{32,64},{64,96},{96,128},{128,160},{160,192},{192,224},{224... | collective-permute-start | bytes 786440 | tf_op jit(solution)/shard_map/while/body/eval_jaxpr/ppermute | solution.py:15
  125.1 10.6 %collective-permute-start = (f32[512,128]{1,0:T(8,128)S(1)}, f32[512,128]{1,0:T(8,128)S(1)}, u32[]{:S(2)}, u32[]{:S(2)}) collective-permute-start(f32[512,128]{1,0:T(8,128)S(1)} %broadcast_select_fusion.3), channel_id=1, source_target_pairs={{0,32},{32,64},{64,96},{96,128},{128,160},{160,192},{192,224},{224... | collective-permute-start | bytes 786440 | tf_op jit(solution)/shard_map/while/body/eval_jaxpr/ppermute | solution.py:15
  138.0 11.8 %collective-permute-start = (f32[512,128]{1,0:T(8,128)S(1)}, f32[512,128]{1,0:T(8,128)S(1)}, u32[]{:S(2)}, u32[]{:S(2)}) collective-permute-start(f32[512,128]{1,0:T(8,128)S(1)} %broadcast_select_fusion.3), channel_id=1, source_target_pairs={{0,32},{32,64},{64,96},{96,128},{128,160},{160,192},{192,224},{224... | collective-permute-start | bytes 786440 | tf_op jit(solution)/shard_map/while/body/eval_jaxpr/ppermute | solution.py:15
  152.0 11.6 %collective-permute-start = (f32[512,128]{1,0:T(8,128)S(1)}, f32[512,128]{1,0:T(8,128)S(1)}, u32[]{:S(2)}, u32[]{:S(2)}) collective-permute-start(f32[512,128]{1,0:T(8,128)S(1)} %broadcast_select_fusion.3), channel_id=1, source_target_pairs={{0,32},{32,64},{64,96},{96,128},{128,160},{160,192},{192,224},{224... | collective-permute-start | bytes 786440 | tf_op jit(solution)/shard_map/while/body/eval_jaxpr/ppermute | solution.py:15
  165.9 10.8 %collective-permute-start = (f32[512,128]{1,0:T(8,128)S(1)}, f32[512,128]{1,0:T(8,128)S(1)}, u32[]{:S(2)}, u32[]{:S(2)}) collective-permute-start(f32[512,128]{1,0:T(8,128)S(1)} %broadcast_select_fusion.3), channel_id=1, source_target_pairs={{0,32},{32,64},{64,96},{96,128},{128,160},{160,192},{192,224},{224... | collective-permute-start | bytes 786440 | tf_op jit(solution)/shard_map/while/body/eval_jaxpr/ppermute | solution.py:15
  179.0 9.9 %collective-permute-start = (f32[512,128]{1,0:T(8,128)S(1)}, f32[512,128]{1,0:T(8,128)S(1)}, u32[]{:S(2)}, u32[]{:S(2)}) collective-permute-start(f32[512,128]{1,0:T(8,128)S(1)} %broadcast_select_fusion.3), channel_id=1, source_target_pairs={{0,32},{32,64},{64,96},{96,128},{128,160},{160,192},{192,224},{224... | collective-permute-start | bytes 786440 | tf_op jit(solution)/shard_map/while/body/eval_jaxpr/ppermute | solution.py:15
  191.1 9.5 %collective-permute-start = (f32[512,128]{1,0:T(8,128)S(1)}, f32[512,128]{1,0:T(8,128)S(1)}, u32[]{:S(2)}, u32[]{:S(2)}) collective-permute-start(f32[512,128]{1,0:T(8,128)S(1)} %broadcast_select_fusion.3), channel_id=1, source_target_pairs={{0,32},{32,64},{64,96},{96,128},{128,160},{160,192},{192,224},{224... | collective-permute-start | bytes 786440 | tf_op jit(solution)/shard_map/while/body/eval_jaxpr/ppermute | solution.py:15
  202.9 9.5 %collective-permute-start = (f32[512,128]{1,0:T(8,128)S(1)}, f32[512,128]{1,0:T(8,128)S(1)}, u32[]{:S(2)}, u32[]{:S(2)}) collective-permute-start(f32[512,128]{1,0:T(8,128)S(1)} %broadcast_select_fusion.3), channel_id=1, source_target_pairs={{0,32},{32,64},{64,96},{96,128},{128,160},{160,192},{192,224},{224... | collective-permute-start | bytes 786440 | tf_op jit(solution)/shard_map/while/body/eval_jaxpr/ppermute | solution.py:15
  214.6 9.5 %collective-permute-start = (f32[512,128]{1,0:T(8,128)S(1)}, f32[512,128]{1,0:T(8,128)S(1)}, u32[]{:S(2)}, u32[]{:S(2)}) collective-permute-start(f32[512,128]{1,0:T(8,128)S(1)} %broadcast_select_fusion.3), channel_id=1, source_target_pairs={{0,32},{32,64},{64,96},{96,128},{128,160},{160,192},{192,224},{224... | collective-permute-start | bytes 786440 | tf_op jit(solution)/shard_map/while/body/eval_jaxpr/ppermute | solution.py:15
  226.3 21.2 %copy-start.1 = (f32[512,128]{1,0:T(8,128)}, f32[512,128]{1,0:T(8,128)S(1)}, u32[]{:S(2)}) copy-start(f32[512,128]{1,0:T(8,128)S(1)} %get-tuple-element.25) | copy-start | bytes 786436
  228.7 19.5 %copy-start.3 = (bf16[128,128]{1,0:T(8,128)(2,1)}, bf16[128,128]{1,0:T(8,128)(2,1)S(1)}, u32[]{:S(2)}) copy-start(bf16[128,128]{1,0:T(8,128)(2,1)S(1)} %fusion.3) | copy-start | bytes 98308
  228.7 18.1 %collective-permute-start.4 = (bf16[128,128]{1,0:T(8,128)(2,1)S(1)}, bf16[128,128]{1,0:T(8,128)(2,1)S(1)}, u32[]{:S(2)}, u32[]{:S(2)}) collective-permute-start(bf16[128,128]{1,0:T(8,128)(2,1)S(1)} %fusion.3), channel_id=1, source_target_pairs={{0,30},{1,31},{2,0},{3,1},{4,2},{5,3},{6,4},{7,5},{8,6},{9,7},{10,... | collective-permute-start | bytes 98312 | tf_op jit(solution)/shard_map/ppermute | solution.py:9
  233.3 13.5 %collective-permute-start.3 = (bf16[128,128]{1,0:T(8,128)(2,1)S(1)}, bf16[128,128]{1,0:T(8,128)(2,1)S(1)}, u32[]{:S(2)}, u32[]{:S(2)}) collective-permute-start(bf16[128,128]{1,0:T(8,128)(2,1)S(1)} %fusion.3), channel_id=1, source_target_pairs={{0,31},{1,0},{2,1},{3,2},{4,3},{5,4},{6,5},{7,6},{8,7},{9,8},{10,9... | collective-permute-start | bytes 98312 | tf_op jit(solution)/shard_map/ppermute | solution.py:9
  235.2 11.5 %collective-permute-start.2 = (bf16[128,128]{1,0:T(8,128)(2,1)S(1)}, bf16[128,128]{1,0:T(8,128)(2,1)S(1)}, u32[]{:S(2)}, u32[]{:S(2)}) collective-permute-start(bf16[128,128]{1,0:T(8,128)(2,1)S(1)} %fusion.3), channel_id=1, source_target_pairs={{0,1},{1,2},{2,3},{3,4},{4,5},{5,6},{6,7},{7,8},{8,9},{9,10},{10,1... | collective-permute-start | bytes 98312 | tf_op jit(solution)/shard_map/ppermute | solution.py:9
  237.7 9.1 %collective-permute-start.1 = (bf16[128,128]{1,0:T(8,128)(2,1)S(1)}, bf16[128,128]{1,0:T(8,128)(2,1)S(1)}, u32[]{:S(2)}, u32[]{:S(2)}) collective-permute-start(bf16[128,128]{1,0:T(8,128)(2,1)S(1)} %fusion.3), channel_id=1, source_target_pairs={{0,2},{1,3},{2,4},{3,5},{4,6},{5,7},{6,8},{7,9},{8,10},{9,11},{10,... | collective-permute-start | bytes 98312 | tf_op jit(solution)/shard_map/ppermute | solution.py:9
where the time goes:
time: 251 us; the launch traced here: 249 us
  waiting for transfers between devices  137 us (55%)
  starting transfers between devices  42.7 us (17%)
  matrix products  39.9 us (16%)
  blocking collectives  25.2 us (10%)
    ppermute x16, waiting for transfers between devices, from_behind_2(): lax.ppermute(value, axis, [(source, source + steps) for source in range(f...  131 us
    dot_general x16, matrix products, relay(): return top_own + jnp.dot(chain_matrix, earlier, precision=highest)  35.4 us
    ppermute x16, starting transfers between devices, from_behind_2(): lax.ppermute(value, axis, [(source, source + steps) for source in range(f...  31.9 us
    all_gather x1, blocking collectives, body(): top_own = lax.all_gather(rows_own, 'sub', axis=0, tiled=True)  25.2 us
    ppermute x4, starting transfers between devices, from_behind(): lax.ppermute(shard, axis, [(i, (i + by) % peers) for i in range(peers)])  10.8 us
    ppermute x4, waiting for transfers between devices, from_behind(): lax.ppermute(shard, axis, [(i, (i + by) % peers) for i in range(peers)])  6 us
  transfers between devices with their start and end apart: 20, of which 17 were waited for; matrix products, arithmetic and copies ran while one was open for 0% of the time, Pallas kernels for 0%

commit v1 on v0

--- a/solution.py
+++ b/solution.py
@@ -45,7 +45,9 @@
     highest = lax.Precision.HIGHEST
     rows_own = jnp.dot(top_basis[0], top_coeffs[0], preferred_element_type=jnp.float32)
     chain_matrix = top_coupling[0]
-    top_own = lax.all_gather(rows_own, "sub", axis=0, tiled=True)
+    top_own = jnp.concatenate(
+        lax.all_to_all(jnp.stack([rows_own] * lax.axis_size("sub")), "sub", 0, 0), axis=0
+    )
     top_field = run_chain(top_own, chain_matrix)
     own_block = jnp.dot(block_basis[0, 0], block_coeffs[0, 0], preferred_element_type=jnp.float32)
     from_top = jnp.dot(block_coupling[0, 0], top_field, precision=highest)

time: 251 us -> 237 us (0.944)
  the two profiles are of different devices: /device:TPU:384 before, /device:TPU:256 now
where the time goes in v1:
time: 237 us
  waiting for transfers between devices  145 us (61%)
  starting transfers between devices  52.3 us (22%)
  matrix products  21.7 us (9%)
  other arithmetic  13 us (5%)
    ppermute x16, waiting for transfers between devices, from_behind_2(): lax.ppermute(value, axis, [(source, source + steps) for source in range(f...  135 us
    ppermute x16, starting transfers between devices, from_behind_2(): lax.ppermute(value, axis, [(source, source + steps) for source in range(f...  31.5 us
    dot_general x16, matrix products, relay(): return top_own + jnp.dot(chain_matrix, earlier, precision=highest)  15.8 us
    ppermute x4, starting transfers between devices, from_behind(): lax.ppermute(shard, axis, [(i, (i + by) % peers) for i in range(peers)])  13.5 us
    while x16, other arithmetic  11.6 us
    all_to_all x1, starting transfers between devices, body(): lax.all_to_all(jnp.stack([rows_own] * lax.axis_size('sub')), 'sub', 0, 0)  7.32 us
    ppermute x4, waiting for transfers between devices, from_behind(): lax.ppermute(shard, axis, [(i, (i + by) % peers) for i in range(peers)])  6.12 us
  transfers between devices with their start and end apart: 21, of which 18 were waited for; matrix products, arithmetic and copies ran while one was open for 2% of the time, Pallas kernels for 0%

profile of v1, /device:TPU:256, one launch (start us, length us, event | category | flops | bytes accessed | tf_op | source)
XLA Modules:
  0.0 236.7 jit_solution(6276279531791011911)
XLA Ops:
  0.7 1.1 fusion.8
  2.5 7.3 %all-to-all-start = ((f32[32,16,128]{2,1,0:T(8,128)}), f32[32,16,128]{2,1,0:T(8,128)S(1)}, u32[]{:S(2)}, u32[]{:S(2)}) async-start(f32[32,16,128]{2,1,0:T(8,128)} %stack.14), calls=%async_computation | async-start | bytes 524288 | tf_op jit(solution)/shard_map/all_to_all | solution.py:49
  11.8 2.6 %fusion.4 = f32[128,1536]{1,0:T(8,128)} fusion(bf16[1,1,1536,256]{3,2,1,0:T(8,128)(2,1)} %param.19, bf16[1,1,256,128]{3,2,1,0:T(8,128)(2,1)} %param.20, pred[256]{0:T(512)(128)(4,1)S(1)} %iota_compare_fusion), kind=kOutput, calls=%fused_computation.10 | convolution fusion | flops 100696064 | bytes 1638656 | tf_op jit(solution)/shard_map/dot_general | solution.py:69
  14.4 4.4 %all-to-all-done = f32[32,16,128]{2,1,0:T(8,128)S(1)} async-done(((f32[32,16,128]{2,1,0:T(8,128)}), f32[32,16,128]{2,1,0:T(8,128)S(1)}, u32[]{:S(2)}, u32[]{:S(2)}) %all-to-all-start) | async-done | bytes 262176 | tf_op jit(solution)/shard_map/all_to_all | solution.py:49
  18.8 194.2 %while.11 = (s32[]{:T(128)}, f32[512,128]{1,0:T(8,128)S(1)}, f32[512,512]{1,0:T(8,128)S(1)}, f32[512,128]{1,0:T(8,128)S(1)}, s32[]{:T(128)}, /*index=5*/s32[]{:T(128)}) while((s32[]{:T(128)}, f32[512,128]{1,0:T(8,128)S(1)}, f32[512,512]{1,0:T(8,128)S(1)}, f32[512,128]{1,0:T(8,128)S(1)}, s32[]{:T(128)}, /*index=5*/s32[]{:T(128)}) %tuple.31), condition=%wide.region_1.0_spmd.clone, body=%wide.region_0.0_spmd.clone.sunk | while | flops 402784256 | bytes 3407991 | solution.py:29
  19.5 2.9 %collective-permute-start = (f32[512,128]{1,0:T(8,128)}, f32[512,128]{1,0:T(8,128)S(1)}, u32[]{:S(2)}, u32[]{:S(2)}) collective-permute-start(f32[512,128]{1,0:T(8,128)} %broadcast_select_fusion.3), channel_id=1, source_target_pairs={{0,32},{32,64},{64,96},{96,128},{128,160},{160,192},{192,224},{224... | collective-permute-start | bytes 786440 | tf_op jit(solution)/shard_map/while/body/eval_jaxpr/ppermute | solution.py:15
  22.4 8.9 %collective-permute-done = f32[512,128]{1,0:T(8,128)S(1)} collective-permute-done((f32[512,128]{1,0:T(8,128)}, f32[512,128]{1,0:T(8,128)S(1)}, u32[]{:S(2)}, u32[]{:S(2)}) %collective-permute-start) | collective-permute-done | bytes 262176 | tf_op jit(solution)/shard_map/while/body/eval_jaxpr/ppermute | solution.py:15
  31.3 1.0 convolution_add_fusion.4
  33.1 1.9 collective-permute-start
  35.0 9.1 %collective-permute-done = f32[512,128]{1,0:T(8,128)S(1)} collective-permute-done((f32[512,128]{1,0:T(8,128)}, f32[512,128]{1,0:T(8,128)S(1)}, u32[]{:S(2)}, u32[]{:S(2)}) %collective-permute-start) | collective-permute-done | bytes 262176 | tf_op jit(solution)/shard_map/while/body/eval_jaxpr/ppermute | solution.py:15
  45.8 1.9 collective-permute-start
  47.7 8.2 %collective-permute-done = f32[512,128]{1,0:T(8,128)S(1)} collective-permute-done((f32[512,128]{1,0:T(8,128)}, f32[512,128]{1,0:T(8,128)S(1)}, u32[]{:S(2)}, u32[]{:S(2)}) %collective-permute-start) | collective-permute-done | bytes 262176 | tf_op jit(solution)/shard_map/while/body/eval_jaxpr/ppermute | solution.py:15
  57.6 1.9 collective-permute-start
  59.5 7.8 %collective-permute-done = f32[512,128]{1,0:T(8,128)S(1)} collective-permute-done((f32[512,128]{1,0:T(8,128)}, f32[512,128]{1,0:T(8,128)S(1)}, u32[]{:S(2)}, u32[]{:S(2)}) %collective-permute-start) | collective-permute-done | bytes 262176 | tf_op jit(solution)/shard_map/while/body/eval_jaxpr/ppermute | solution.py:15
  67.3 1.0 convolution_add_fusion.4
  69.0 1.9 collective-permute-start
  70.9 7.8 %collective-permute-done = f32[512,128]{1,0:T(8,128)S(1)} collective-permute-done((f32[512,128]{1,0:T(8,128)}, f32[512,128]{1,0:T(8,128)S(1)}, u32[]{:S(2)}, u32[]{:S(2)}) %collective-permute-start) | collective-permute-done | bytes 262176 | tf_op jit(solution)/shard_map/while/body/eval_jaxpr/ppermute | solution.py:15
  80.4 1.9 collective-permute-start
  82.3 7.8 %collective-permute-done = f32[512,128]{1,0:T(8,128)S(1)} collective-permute-done((f32[512,128]{1,0:T(8,128)}, f32[512,128]{1,0:T(8,128)S(1)}, u32[]{:S(2)}, u32[]{:S(2)}) %collective-permute-start) | collective-permute-done | bytes 262176 | tf_op jit(solution)/shard_map/while/body/eval_jaxpr/ppermute | solution.py:15
  91.8 1.9 collective-permute-start
  93.7 7.8 %collective-permute-done = f32[512,128]{1,0:T(8,128)S(1)} collective-permute-done((f32[512,128]{1,0:T(8,128)}, f32[512,128]{1,0:T(8,128)S(1)}, u32[]{:S(2)}, u32[]{:S(2)}) %collective-permute-start) | collective-permute-done | bytes 262176 | tf_op jit(solution)/shard_map/while/body/eval_jaxpr/ppermute | solution.py:15
  101.5 1.0 convolution_add_fusion.4
  103.2 1.9 collective-permute-start
  105.1 8.1 %collective-permute-done = f32[512,128]{1,0:T(8,128)S(1)} collective-permute-done((f32[512,128]{1,0:T(8,128)}, f32[512,128]{1,0:T(8,128)S(1)}, u32[]{:S(2)}, u32[]{:S(2)}) %collective-permute-start) | collective-permute-done | bytes 262176 | tf_op jit(solution)/shard_map/while/body/eval_jaxpr/ppermute | solution.py:15
  113.3 1.0 convolution_add_fusion.4
  115.0 1.9 collective-permute-start
  116.9 9.3 %collective-permute-done = f32[512,128]{1,0:T(8,128)S(1)} collective-permute-done((f32[512,128]{1,0:T(8,128)}, f32[512,128]{1,0:T(8,128)S(1)}, u32[]{:S(2)}, u32[]{:S(2)}) %collective-permute-start) | collective-permute-done | bytes 262176 | tf_op jit(solution)/shard_map/while/body/eval_jaxpr/ppermute | solution.py:15
  127.9 1.9 collective-permute-start
  129.8 10.4 %collective-permute-done = f32[512,128]{1,0:T(8,128)S(1)} collective-permute-done((f32[512,128]{1,0:T(8,128)}, f32[512,128]{1,0:T(8,128)S(1)}, u32[]{:S(2)}, u32[]{:S(2)}) %collective-permute-start) | collective-permute-done | bytes 262176 | tf_op jit(solution)/shard_map/while/body/eval_jaxpr/ppermute | solution.py:15
  142.0 1.9 collective-permute-start
  143.9 9.7 %collective-permute-done = f32[512,128]{1,0:T(8,128)S(1)} collective-permute-done((f32[512,128]{1,0:T(8,128)}, f32[512,128]{1,0:T(8,128)S(1)}, u32[]{:S(2)}, u32[]{:S(2)}) %collective-permute-start) | collective-permute-done | bytes 262176 | tf_op jit(solution)/shard_map/while/body/eval_jaxpr/ppermute | solution.py:15
  155.3 1.9 collective-permute-start
  157.3 8.9 %collective-permute-done = f32[512,128]{1,0:T(8,128)S(1)} collective-permute-done((f32[512,128]{1,0:T(8,128)}, f32[512,128]{1,0:T(8,128)S(1)}, u32[]{:S(2)}, u32[]{:S(2)}) %collective-permute-start) | collective-permute-done | bytes 262176 | tf_op jit(solution)/shard_map/while/body/eval_jaxpr/ppermute | solution.py:15
  167.9 1.9 collective-permute-start
  169.8 8.0 %collective-permute-done = f32[512,128]{1,0:T(8,128)S(1)} collective-permute-done((f32[512,128]{1,0:T(8,128)}, f32[512,128]{1,0:T(8,128)S(1)}, u32[]{:S(2)}, u32[]{:S(2)}) %collective-permute-start) | collective-permute-done | bytes 262176 | tf_op jit(solution)/shard_map/while/body/eval_jaxpr/ppermute | solution.py:15
  179.5 1.9 collective-permute-start
  181.4 7.8 %collective-permute-done = f32[512,128]{1,0:T(8,128)S(1)} collective-permute-done((f32[512,128]{1,0:T(8,128)}, f32[512,128]{1,0:T(8,128)S(1)}, u32[]{:S(2)}, u32[]{:S(2)}) %collective-permute-start) | collective-permute-done | bytes 262176 | tf_op jit(solution)/shard_map/while/body/eval_jaxpr/ppermute | solution.py:15
  189.2 1.0 convolution_add_fusion.4
  190.9 1.9 collective-permute-start
  192.8 7.8 %collective-permute-done = f32[512,128]{1,0:T(8,128)S(1)} collective-permute-done((f32[512,128]{1,0:T(8,128)}, f32[512,128]{1,0:T(8,128)S(1)}, u32[]{:S(2)}, u32[]{:S(2)}) %collective-permute-start) | collective-permute-done | bytes 262176 | tf_op jit(solution)/shard_map/while/body/eval_jaxpr/ppermute | solution.py:15
  202.3 1.9 collective-permute-start
  204.2 7.8 %collective-permute-done = f32[512,128]{1,0:T(8,128)S(1)} collective-permute-done((f32[512,128]{1,0:T(8,128)}, f32[512,128]{1,0:T(8,128)S(1)}, u32[]{:S(2)}, u32[]{:S(2)}) %collective-permute-start) | collective-permute-done | bytes 262176 | tf_op jit(solution)/shard_map/while/body/eval_jaxpr/ppermute | solution.py:15
  213.0 1.5 convolution_bitcast_fusion
  214.6 2.4 %collective-permute-start.1 = (bf16[128,128]{1,0:T(8,128)(2,1)S(1)}, bf16[128,128]{1,0:T(8,128)(2,1)S(1)}, u32[]{:S(2)}, u32[]{:S(2)}) collective-permute-start(bf16[128,128]{1,0:T(8,128)(2,1)S(1)} %fusion.3), channel_id=1, source_target_pairs={{0,2},{1,3},{2,4},{3,5},{4,6},{5,7},{6,8},{7,9},{8,10},{9,11},{10,... | collective-permute-start | bytes 98312 | tf_op jit(solution)/shard_map/ppermute | solution.py:9
  217.1 6.7 %collective-permute-start.4 = (bf16[128,128]{1,0:T(8,128)(2,1)S(1)}, bf16[128,128]{1,0:T(8,128)(2,1)S(1)}, u32[]{:S(2)}, u32[]{:S(2)}) collective-permute-start(bf16[128,128]{1,0:T(8,128)(2,1)S(1)} %fusion.3), channel_id=1, source_target_pairs={{0,30},{1,31},{2,0},{3,1},{4,2},{5,3},{6,4},{7,5},{8,6},{9,7},{10,... | collective-permute-start | bytes 98312 | tf_op jit(solution)/shard_map/ppermute | solution.py:9
  223.8 1.9 collective-permute-start.3
  225.8 2.4 %collective-permute-start.2 = (bf16[128,128]{1,0:T(8,128)(2,1)S(1)}, bf16[128,128]{1,0:T(8,128)(2,1)S(1)}, u32[]{:S(2)}, u32[]{:S(2)}) collective-permute-start(bf16[128,128]{1,0:T(8,128)(2,1)S(1)} %fusion.3), channel_id=1, source_target_pairs={{0,1},{1,2},{2,3},{3,4},{4,5},{5,6},{6,7},{7,8},{8,9},{9,10},{10,1... | collective-permute-start | bytes 98312 | tf_op jit(solution)/shard_map/ppermute | solution.py:9
  228.2 6.1 %collective-permute-done.2 = bf16[128,128]{1,0:T(8,128)(2,1)S(1)} collective-permute-done((bf16[128,128]{1,0:T(8,128)(2,1)S(1)}, bf16[128,128]{1,0:T(8,128)(2,1)S(1)}, u32[]{:S(2)}, u32[]{:S(2)}) %collective-permute-start.2) | collective-permute-done | bytes 32800 | tf_op jit(solution)/shard_map/ppermute | solution.py:9
  (60 shorter events, 26.9 us)
Async XLA Ops:
  0.6 234.4 %copy-start = (bf16[1,1,1536,512]{3,2,1,0:T(8,128)(2,1)S(1)}, bf16[1,1,1536,512]{3,2,1,0:T(8,128)(2,1)}, u32[]{:S(2)}) copy-start(bf16[1,1,1536,512]{3,2,1,0:T(8,128)(2,1)} %param.22) | copy-start | bytes 4718596
  0.6 18.1 %copy-start.1 = (f32[1,512,512]{2,1,0:T(8,128)S(1)}, f32[1,512,512]{2,1,0:T(8,128)}, u32[]{:S(2)}) copy-start(f32[1,512,512]{2,1,0:T(8,128)} %param.15) | copy-start | bytes 3145732
  2.5 16.2 %all-to-all-start = ((f32[32,16,128]{2,1,0:T(8,128)}), f32[32,16,128]{2,1,0:T(8,128)S(1)}, u32[]{:S(2)}, u32[]{:S(2)}) async-start(f32[32,16,128]{2,1,0:T(8,128)} %stack.14), calls=%async_computation | async-start | bytes 524288 | tf_op jit(solution)/shard_map/all_to_all | solution.py:49
  18.8 195.7 %copy-start.5 = (bf16[1,1,128,128]{3,2,1,0:T(8,128)(2,1)S(1)}, bf16[1,1,128,128]{3,2,1,0:T(8,128)(2,1)}, u32[]{:S(2)}) copy-start(bf16[1,1,128,128]{3,2,1,0:T(8,128)(2,1)} %param.18) | copy-start | bytes 98308
  18.8 195.7 %copy-start.6 = (bf16[1,1,128,128]{3,2,1,0:T(8,128)(2,1)S(1)}, bf16[1,1,128,128]{3,2,1,0:T(8,128)(2,1)}, u32[]{:S(2)}) copy-start(bf16[1,1,128,128]{3,2,1,0:T(8,128)(2,1)} %param.17) | copy-start | bytes 98308
  19.5 11.8 %collective-permute-start = (f32[512,128]{1,0:T(8,128)}, f32[512,128]{1,0:T(8,128)S(1)}, u32[]{:S(2)}, u32[]{:S(2)}) collective-permute-start(f32[512,128]{1,0:T(8,128)} %broadcast_select_fusion.3), channel_id=1, source_target_pairs={{0,32},{32,64},{64,96},{96,128},{128,160},{160,192},{192,224},{224... | collective-permute-start | bytes 786440 | tf_op jit(solution)/shard_map/while/body/eval_jaxpr/ppermute | solution.py:15
  33.1 11.0 %collective-permute-start = (f32[512,128]{1,0:T(8,128)}, f32[512,128]{1,0:T(8,128)S(1)}, u32[]{:S(2)}, u32[]{:S(2)}) collective-permute-start(f32[512,128]{1,0:T(8,128)} %broadcast_select_fusion.3), channel_id=1, source_target_pairs={{0,32},{32,64},{64,96},{96,128},{128,160},{160,192},{192,224},{224... | collective-permute-start | bytes 786440 | tf_op jit(solution)/shard_map/while/body/eval_jaxpr/ppermute | solution.py:15
  45.8 10.1 %collective-permute-start = (f32[512,128]{1,0:T(8,128)}, f32[512,128]{1,0:T(8,128)S(1)}, u32[]{:S(2)}, u32[]{:S(2)}) collective-permute-start(f32[512,128]{1,0:T(8,128)} %broadcast_select_fusion.3), channel_id=1, source_target_pairs={{0,32},{32,64},{64,96},{96,128},{128,160},{160,192},{192,224},{224... | collective-permute-start | bytes 786440 | tf_op jit(solution)/shard_map/while/body/eval_jaxpr/ppermute | solution.py:15
  57.6 9.7 %collective-permute-start = (f32[512,128]{1,0:T(8,128)}, f32[512,128]{1,0:T(8,128)S(1)}, u32[]{:S(2)}, u32[]{:S(2)}) collective-permute-start(f32[512,128]{1,0:T(8,128)} %broadcast_select_fusion.3), channel_id=1, source_target_pairs={{0,32},{32,64},{64,96},{96,128},{128,160},{160,192},{192,224},{224... | collective-permute-start | bytes 786440 | tf_op jit(solution)/shard_map/while/body/eval_jaxpr/ppermute | solution.py:15
  69.0 9.7 %collective-permute-start = (f32[512,128]{1,0:T(8,128)}, f32[512,128]{1,0:T(8,128)S(1)}, u32[]{:S(2)}, u32[]{:S(2)}) collective-permute-start(f32[512,128]{1,0:T(8,128)} %broadcast_select_fusion.3), channel_id=1, source_target_pairs={{0,32},{32,64},{64,96},{96,128},{128,160},{160,192},{192,224},{224... | collective-permute-start | bytes 786440 | tf_op jit(solution)/shard_map/while/body/eval_jaxpr/ppermute | solution.py:15
  80.4 9.7 %collective-permute-start = (f32[512,128]{1,0:T(8,128)}, f32[512,128]{1,0:T(8,128)S(1)}, u32[]{:S(2)}, u32[]{:S(2)}) collective-permute-start(f32[512,128]{1,0:T(8,128)} %broadcast_select_fusion.3), channel_id=1, source_target_pairs={{0,32},{32,64},{64,96},{96,128},{128,160},{160,192},{192,224},{224... | collective-permute-start | bytes 786440 | tf_op jit(solution)/shard_map/while/body/eval_jaxpr/ppermute | solution.py:15
  91.8 9.7 %collective-permute-start = (f32[512,128]{1,0:T(8,128)}, f32[512,128]{1,0:T(8,128)S(1)}, u32[]{:S(2)}, u32[]{:S(2)}) collective-permute-start(f32[512,128]{1,0:T(8,128)} %broadcast_select_fusion.3), channel_id=1, source_target_pairs={{0,32},{32,64},{64,96},{96,128},{128,160},{160,192},{192,224},{224... | collective-permute-start | bytes 786440 | tf_op jit(solution)/shard_map/while/body/eval_jaxpr/ppermute | solution.py:15
  103.2 10.0 %collective-permute-start = (f32[512,128]{1,0:T(8,128)}, f32[512,128]{1,0:T(8,128)S(1)}, u32[]{:S(2)}, u32[]{:S(2)}) collective-permute-start(f32[512,128]{1,0:T(8,128)} %broadcast_select_fusion.3), channel_id=1, source_target_pairs={{0,32},{32,64},{64,96},{96,128},{128,160},{160,192},{192,224},{224... | collective-permute-start | bytes 786440 | tf_op jit(solution)/shard_map/while/body/eval_jaxpr/ppermute | solution.py:15
  115.0 11.2 %collective-permute-start = (f32[512,128]{1,0:T(8,128)}, f32[512,128]{1,0:T(8,128)S(1)}, u32[]{:S(2)}, u32[]{:S(2)}) collective-permute-start(f32[512,128]{1,0:T(8,128)} %broadcast_select_fusion.3), channel_id=1, source_target_pairs={{0,32},{32,64},{64,96},{96,128},{128,160},{160,192},{192,224},{224... | collective-permute-start | bytes 786440 | tf_op jit(solution)/shard_map/while/body/eval_jaxpr/ppermute | solution.py:15
  127.9 12.3 %collective-permute-start = (f32[512,128]{1,0:T(8,128)}, f32[512,128]{1,0:T(8,128)S(1)}, u32[]{:S(2)}, u32[]{:S(2)}) collective-permute-start(f32[512,128]{1,0:T(8,128)} %broadcast_select_fusion.3), channel_id=1, source_target_pairs={{0,32},{32,64},{64,96},{96,128},{128,160},{160,192},{192,224},{224... | collective-permute-start | bytes 786440 | tf_op jit(solution)/shard_map/while/body/eval_jaxpr/ppermute | solution.py:15
  142.0 11.6 %collective-permute-start = (f32[512,128]{1,0:T(8,128)}, f32[512,128]{1,0:T(8,128)S(1)}, u32[]{:S(2)}, u32[]{:S(2)}) collective-permute-start(f32[512,128]{1,0:T(8,128)} %broadcast_select_fusion.3), channel_id=1, source_target_pairs={{0,32},{32,64},{64,96},{96,128},{128,160},{160,192},{192,224},{224... | collective-permute-start | bytes 786440 | tf_op jit(solution)/shard_map/while/body/eval_jaxpr/ppermute | solution.py:15
  155.3 10.8 %collective-permute-start = (f32[512,128]{1,0:T(8,128)}, f32[512,128]{1,0:T(8,128)S(1)}, u32[]{:S(2)}, u32[]{:S(2)}) collective-permute-start(f32[512,128]{1,0:T(8,128)} %broadcast_select_fusion.3), channel_id=1, source_target_pairs={{0,32},{32,64},{64,96},{96,128},{128,160},{160,192},{192,224},{224... | collective-permute-start | bytes 786440 | tf_op jit(solution)/shard_map/while/body/eval_jaxpr/ppermute | solution.py:15
  167.9 9.9 %collective-permute-start = (f32[512,128]{1,0:T(8,128)}, f32[512,128]{1,0:T(8,128)S(1)}, u32[]{:S(2)}, u32[]{:S(2)}) collective-permute-start(f32[512,128]{1,0:T(8,128)} %broadcast_select_fusion.3), channel_id=1, source_target_pairs={{0,32},{32,64},{64,96},{96,128},{128,160},{160,192},{192,224},{224... | collective-permute-start | bytes 786440 | tf_op jit(solution)/shard_map/while/body/eval_jaxpr/ppermute | solution.py:15
  179.5 9.7 %collective-permute-start = (f32[512,128]{1,0:T(8,128)}, f32[512,128]{1,0:T(8,128)S(1)}, u32[]{:S(2)}, u32[]{:S(2)}) collective-permute-start(f32[512,128]{1,0:T(8,128)} %broadcast_select_fusion.3), channel_id=1, source_target_pairs={{0,32},{32,64},{64,96},{96,128},{128,160},{160,192},{192,224},{224... | collective-permute-start | bytes 786440 | tf_op jit(solution)/shard_map/while/body/eval_jaxpr/ppermute | solution.py:15
  190.9 9.7 %collective-permute-start = (f32[512,128]{1,0:T(8,128)}, f32[512,128]{1,0:T(8,128)S(1)}, u32[]{:S(2)}, u32[]{:S(2)}) collective-permute-start(f32[512,128]{1,0:T(8,128)} %broadcast_select_fusion.3), channel_id=1, source_target_pairs={{0,32},{32,64},{64,96},{96,128},{128,160},{160,192},{192,224},{224... | collective-permute-start | bytes 786440 | tf_op jit(solution)/shard_map/while/body/eval_jaxpr/ppermute | solution.py:15
  202.3 9.7 %collective-permute-start = (f32[512,128]{1,0:T(8,128)}, f32[512,128]{1,0:T(8,128)S(1)}, u32[]{:S(2)}, u32[]{:S(2)}) collective-permute-start(f32[512,128]{1,0:T(8,128)} %broadcast_select_fusion.3), channel_id=1, source_target_pairs={{0,32},{32,64},{64,96},{96,128},{128,160},{160,192},{192,224},{224... | collective-permute-start | bytes 786440 | tf_op jit(solution)/shard_map/while/body/eval_jaxpr/ppermute | solution.py:15
  213.0 22.7 %copy-start.2 = (f32[512,128]{1,0:T(8,128)}, f32[512,128]{1,0:T(8,128)S(1)}, u32[]{:S(2)}) copy-start(f32[512,128]{1,0:T(8,128)S(1)} %get-tuple-element.25) | copy-start | bytes 786436
  213.0 22.1 %copy-start.3 = (f32[128,1536]{1,0:T(8,128)S(1)}, f32[128,1536]{1,0:T(8,128)}, u32[]{:S(2)}) copy-start(f32[128,1536]{1,0:T(8,128)} %fusion.4) | copy-start | bytes 2359300
  214.6 21.1 %copy-start.4 = (bf16[128,128]{1,0:T(8,128)(2,1)}, bf16[128,128]{1,0:T(8,128)(2,1)S(1)}, u32[]{:S(2)}) copy-start(bf16[128,128]{1,0:T(8,128)(2,1)S(1)} %fusion.3) | copy-start | bytes 98308
  214.6 13.5 %collective-permute-start.1 = (bf16[128,128]{1,0:T(8,128)(2,1)S(1)}, bf16[128,128]{1,0:T(8,128)(2,1)S(1)}, u32[]{:S(2)}, u32[]{:S(2)}) collective-permute-start(bf16[128,128]{1,0:T(8,128)(2,1)S(1)} %fusion.3), channel_id=1, source_target_pairs={{0,2},{1,3},{2,4},{3,5},{4,6},{5,7},{6,8},{7,9},{8,10},{9,11},{10,... | collective-permute-start | bytes 98312 | tf_op jit(solution)/shard_map/ppermute | solution.py:9
  217.1 17.3 %collective-permute-start.4 = (bf16[128,128]{1,0:T(8,128)(2,1)S(1)}, bf16[128,128]{1,0:T(8,128)(2,1)S(1)}, u32[]{:S(2)}, u32[]{:S(2)}) collective-permute-start(bf16[128,128]{1,0:T(8,128)(2,1)S(1)} %fusion.3), channel_id=1, source_target_pairs={{0,30},{1,31},{2,0},{3,1},{4,2},{5,3},{6,4},{7,5},{8,6},{9,7},{10,... | collective-permute-start | bytes 98312 | tf_op jit(solution)/shard_map/ppermute | solution.py:9
  223.8 10.5 %collective-permute-start.3 = (bf16[128,128]{1,0:T(8,128)(2,1)S(1)}, bf16[128,128]{1,0:T(8,128)(2,1)S(1)}, u32[]{:S(2)}, u32[]{:S(2)}) collective-permute-start(bf16[128,128]{1,0:T(8,128)(2,1)S(1)} %fusion.3), channel_id=1, source_target_pairs={{0,31},{1,0},{2,1},{3,2},{4,3},{5,4},{6,5},{7,6},{8,7},{9,8},{10,9... | collective-permute-start | bytes 98312 | tf_op jit(solution)/shard_map/ppermute | solution.py:9
  225.8 8.6 %collective-permute-start.2 = (bf16[128,128]{1,0:T(8,128)(2,1)S(1)}, bf16[128,128]{1,0:T(8,128)(2,1)S(1)}, u32[]{:S(2)}, u32[]{:S(2)}) collective-permute-start(bf16[128,128]{1,0:T(8,128)(2,1)S(1)} %fusion.3), channel_id=1, source_target_pairs={{0,1},{1,2},{2,3},{3,4},{4,5},{5,6},{6,7},{7,8},{8,9},{9,10},{10,1... | collective-permute-start | bytes 98312 | tf_op jit(solution)/shard_map/ppermute | solution.py:9
